TPU v7x, 32 devices: a whole 2x2x4 slice. The times are simulated.
32 devices in a mesh: rows: 4 (over x, core), cols: 8 (over z, y).
Axes of the slice: x: 2, y: 2, z: 4, core: 2. Of those that a mesh axis runs over, the one named last changes fastest.
Arguments:
- tensor: float32 [48, 256, 512], P('rows', 'cols'), may hold values from 0 to 1
- first_factor: float32 [48, 256], P('rows', 'cols'), may hold values from -2.5 to 2.5
- second_factor: float32 [256, 256], P('cols', 'rows'), may hold values from -2.5 to 2.5
- third_factor: float32 [512, 256], P(('rows', 'cols')), may hold values from -2.5 to 2.5
Outputs:
- first_new: float32 [48, 256], P('rows', 'cols')
- second_new: float32 [256, 256], P('cols', 'rows')
- third_new: float32 [512, 256], P(('rows', 'cols'))
All inputs are finite; a program needn't handle non-finite values.
Results may differ from a plain program's by a relative error of at most 0.0003.
Values sent between devices are 32-bit elements; how exact they have to be, the bound alone decides.
A program may use at most 64 MiB of HBM per device.

v0:
```python
import jax
import jax.numpy as jnp
from jax import lax
from jax.sharding import PartitionSpec as P

STEPS = 2


def gather_third(piece):
    return lax.all_gather(piece, ("rows", "cols"), axis=0, tiled=True)


def per_device(tensor, first_factor, second_factor, third_factor):
    high = lax.Precision.HIGHEST
    rows_dev, cols_dev, depth = tensor.shape
    size_i = rows_dev * lax.axis_size("rows")
    size_j = cols_dev * lax.axis_size("cols")
    rate_a = 4.0 / jnp.sqrt(jnp.float32(size_j * depth))
    rate_b = 4.0 / jnp.sqrt(jnp.float32(size_i * depth))
    rate_c = 4.0 / jnp.sqrt(jnp.float32(size_i * size_j))
    flat_target = tensor.reshape(-1, depth)
    shard_a, shard_b = (first_factor, second_factor)
    whole_c = gather_third(third_factor)
    for step_index in range(STEPS):
        whole_a = lax.all_gather(shard_a, "cols", axis=1, tiled=True)
        whole_b = lax.all_gather(shard_b, "rows", axis=1, tiled=True)
        khatri = (whole_a[:, None, :] * whole_b[None, :, :]).reshape(-1, whole_a.shape[1])
        model_tile = jnp.dot(khatri, whole_c.T, precision=high, preferred_element_type=jnp.float32)
        deriv = jax.nn.sigmoid(model_tile) - flat_target
        deriv_c = jnp.dot(
            deriv, whole_c, precision=high, preferred_element_type=jnp.float32
        ).reshape(rows_dev, cols_dev, -1)
        term_a = jnp.einsum("ijr,jr->ir", deriv_c, whole_b, precision=high)
        term_b = jnp.einsum("ijr,ir->jr", deriv_c, whole_a, precision=high)
        term_c = lax.dot_general(
            deriv,
            khatri,
            (((0,), (0,)), ((), ())),
            precision=high,
            preferred_element_type=jnp.float32,
        )
        shard_a = shard_a - rate_a * lax.psum_scatter(
            term_a, "cols", scatter_dimension=1, tiled=True
        )
        shard_b = shard_b - rate_b * lax.psum_scatter(
            term_b, "rows", scatter_dimension=1, tiled=True
        )
        whole_c = whole_c - rate_c * lax.psum(term_c, ("rows", "cols"))
    owner = lax.axis_index("rows") * lax.axis_size("cols") + lax.axis_index("cols")
    count = third_factor.shape[0]
    shard_c = lax.dynamic_slice_in_dim(whole_c, owner * count, count, 0)
    return (shard_a, shard_b, shard_c)


def solution(mesh):
    in_specs = (
        P("rows", "cols", None),
        P("rows", "cols"),
        P("cols", "rows"),
        P(("rows", "cols"), None),
    )
    out_specs = (P("rows", "cols"), P("cols", "rows"), P(("rows", "cols"), None))
    return jax.shard_map(
        per_device, mesh=mesh, in_specs=in_specs, out_specs=out_specs, check_vma=False
    )
```

profile of v0, /device:TPU:0, one launch (start us, length us, event | category | flops | bytes accessed | tf_op | source)
XLA Modules:
  0.0 396.7 jit_solution(13207134595895252881)
XLA Ops:
  8.0 6.5 %all-gather.1 = f32[4,64,32]{1,2,0:T(8,128)S(1)} all-gather(f32[1,64,32]{1,2,0:T(8,128)} %bitcast.87), channel_id=1, replica_groups=mesh['rows'=4,'cols'=8] {'rows'}, dimensions={0}, use_global_device_ids=true | all-gather | bytes 40960 | tf_op jit(solution)/shard_map/all_gather | solution.py:26
  15.2 31.3 %all-gather = f32[8,32,12]{1,2,0:T(8,128)S(1)} all-gather(f32[1,32,12]{1,2,0:T(8,128)S(1)} %bitcast.90), channel_id=1, replica_groups=mesh['rows'=4,'cols'=8] {'cols'}, dimensions={0}, use_global_device_ids=true | all-gather | bytes 13824 | tf_op jit(solution)/shard_map/all_gather | solution.py:25
  47.3 68.2 %all_gather.17 = f32[512,256]{1,0:T(8,128)S(1)} all-gather(f32[16,256]{1,0:T(8,128)S(1)} %copy-done.2), channel_id=1, replica_groups=mesh['rows'=4,'cols'=8] {'rows','cols'}, dimensions={0}, use_global_device_ids=true | all-gather | bytes 540672 | tf_op jit(solution)/shard_map/all_gather | solution.py:10
  115.6 0.9 fusion.7
  116.5 0.8 fusion.10
  117.4 0.8 copy.42
  119.1 2.3 fusion.11
  121.4 55.9 %reduce-scatter.13.cloned.1.call-done = f32[32,12]{1,0:T(8,128)} async-done(((f32[256,12]{1,0:T(8,128)}), f32[32,12]{1,0:T(8,128)}) %reduce-scatter.13.cloned.1.call-update) | async-done | bytes 1552
  177.3 0.8 copy.43
  178.1 30.5 %all-gather.3 = f32[8,32,12]{1,2,0:T(8,128)S(1)} all-gather(f32[1,32,12]{1,2,0:T(8,128)S(1)} %fusion.9), channel_id=1, replica_groups=mesh['rows'=4,'cols'=8] {'cols'}, dimensions={0}, use_global_device_ids=true | all-gather | bytes 13824 | tf_op jit(solution)/shard_map/all_gather | solution.py:25
  208.7 0.8 copy.45
  209.6 5.2 %all-gather.2 = f32[4,64,32]{1,2,0:T(8,128)S(1)} all-gather(f32[1,64,32]{1,2,0:T(8,128)S(1)} %fusion.8), channel_id=1, replica_groups=mesh['rows'=4,'cols'=8] {'rows'}, dimensions={0}, use_global_device_ids=true | all-gather | bytes 40960 | tf_op jit(solution)/shard_map/all_gather | solution.py:26
  215.0 35.3 %all-reduce.3.cloned.1.call-done = f32[512,256]{1,0:T(8,128)} async-done(((f32[512,256]{1,0:T(8,128)}), f32[512,256]{1,0:T(8,128)}) %all-reduce.3.cloned.1.call-update) | async-done | bytes 524304 | tf_op jit(solution)/shard_map/psum | solution.py:48
  250.3 1.2 multiply_subtract_fusion
  251.5 0.9 fusion.6
  252.4 0.8 fusion.12
  253.2 0.8 copy.46
  255.0 2.2 fusion.13
  257.2 58.0 %reduce-scatter.17.cloned.1.call-done = f32[32,12]{1,0:T(8,128)} async-done(((f32[256,12]{1,0:T(8,128)}), f32[32,12]{1,0:T(8,128)}) %reduce-scatter.17.cloned.1.call-update) | async-done | bytes 1552
  315.2 0.8 copy.47
  316.6 19.6 %reduce-scatter.19.cloned.1.call-done = f32[64,32]{1,0:T(8,128)} async-done(((f32[256,32]{1,0:T(8,128)}), f32[64,32]{1,0:T(8,128)}) %reduce-scatter.19.cloned.1.call-update) | async-done | bytes 8208
  336.2 0.8 copy.49
  337.6 50.6 %all-reduce.5.cloned.1.call-done = f32[512,256]{1,0:T(8,128)} async-done(((f32[512,256]{1,0:T(8,128)}), f32[512,256]{1,0:T(8,128)}) %all-reduce.5.cloned.1.call-update) | async-done | bytes 524304 | tf_op jit(solution)/shard_map/psum | solution.py:48
  388.2 1.3 dynamic-slice_subtract_fusion
  (41 shorter events, 5.1 us)
Async XLA Ops:
  8.0 169.3 %reduce-scatter.13.cloned.1.call-start = ((), (), s32[]{:S(2)}) async-start(), calls=%async_computation.6 | async-start | bytes 147456
  14.5 0.7 copy-start.1
  46.6 0.7 copy-start.2
  46.6 68.9 %copy-start.3 = (f32[12,32,512]{2,1,0:T(8,128)S(1)}, f32[12,32,512]{2,1,0:T(8,128)}, u32[]{:S(2)}) copy-start(f32[12,32,512]{2,1,0:T(8,128)} %param.4) | copy-start | bytes 2359300
  118.2 90.6 %reduce-scatter.15.cloned.1.call-start = ((), (), s32[]{:S(2)}) async-start(), calls=%async_computation.7 | async-start | bytes 163840
  119.0 131.3 %all-reduce.3.cloned.1.call-start = ((), (), s32[]{:S(2)}) async-start(), calls=%async_computation.4 | async-start | bytes 1048576 | tf_op jit(solution)/shard_map/psum | solution.py:48
  121.4 193.8 %reduce-scatter.17.cloned.1.call-start = ((), (), s32[]{:S(2)}) async-start(), calls=%async_computation.8 | async-start | bytes 147456
  208.7 0.8 copy-start
  254.0 82.1 %reduce-scatter.19.cloned.1.call-start = ((), (), s32[]{:S(2)}) async-start(), calls=%async_computation.9 | async-start | bytes 163840
  254.9 133.3 %all-reduce.5.cloned.1.call-start = ((), (), s32[]{:S(2)}) async-start(), calls=%async_computation.5 | async-start | bytes 1048576 | tf_op jit(solution)/shard_map/psum | solution.py:48
Sparse Core Ops, SparseCore 0:
  118.3 58.9 reduce-scatter.12
  179.7 18.6 reduce-scatter.14
  254.2 60.9 reduce-scatter.16
  317.5 18.6 reduce-scatter.18
Sparse Core Ops, SparseCore 1:
  124.8 125.5 all-reduce.2
  260.7 127.5 all-reduce.4
where the time goes:
time: 397 us
  waiting for transfers between devices  219 us (55%)
  blocking collectives  142 us (36%)
  between operations  15.4 us (4%)
  local copies, waits for them, and re-layouts  7.98 us (2%)
  matrix products  7.96 us (2%)
  other arithmetic  3.99 us (1%)
    unnamed x10, waiting for transfers between devices  133 us
    psum x2, waiting for transfers between devices, per_device(): whole_c = whole_c - rate_c * lax.psum(term_c, ('rows', 'cols'))  85.9 us
    all_gather x1, blocking collectives, gather_third(): return lax.all_gather(piece, ('rows', 'cols'), axis=0, tiled=True)  68.2 us
    all_gather x2, blocking collectives, per_device(): whole_a = lax.all_gather(shard_a, 'cols', axis=1, tiled=True)  61.9 us
    all_gather x2, blocking collectives, per_device(): whole_b = lax.all_gather(shard_b, 'rows', axis=1, tiled=True)  11.7 us
  transfers between devices with their start and end apart: 6, of which 5 were waited for; matrix products, arithmetic and copies ran while one was open for 3% of the time, Pallas kernels for 0%

commit v1 on v0

--- a/solution.py
+++ b/solution.py
@@ -45,7 +45,7 @@
         shard_b = shard_b - rate_b * lax.psum_scatter(
             term_b, "rows", scatter_dimension=1, tiled=True
         )
-        whole_c = whole_c - rate_c * lax.psum(term_c, ("rows", "cols"))
+        whole_c = whole_c - rate_c * lax.psum(lax.psum(term_c, "cols"), "rows")
     owner = lax.axis_index("rows") * lax.axis_size("cols") + lax.axis_index("cols")
     count = third_factor.shape[0]
     shard_c = lax.dynamic_slice_in_dim(whole_c, owner * count, count, 0)

time: 397 us -> 515 us (1.30)
  waiting for transfers between devices: 219 us -> 338 us
    psum x2 -> x4, waiting for transfers between devices: 85.9 us -> 202 us  [per_device(): whole_c = whole_c - rate_c * lax.psum(lax.psum(term_c, 'cols'), 'rows')]
    unnamed x10 -> x12, waiting for transfers between devices: 133 us -> 136 us
  transfers between devices with their start and end apart: 6 -> 8, of which waited for: 5 -> 7; matrix products, arithmetic and copies ran while one was open for 3% -> 2% of each run, Pallas kernels for 0% -> 0%
where the time goes in v1:
time: 515 us
  waiting for transfers between devices  338 us (66%)
  blocking collectives  142 us (28%)
  between operations  14.3 us (3%)
  local copies, waits for them, and re-layouts  8.61 us (2%)
  matrix products  7.92 us (2%)
    psum x4, waiting for transfers between devices, per_device(): whole_c = whole_c - rate_c * lax.psum(lax.psum(term_c, 'cols'), 'rows')  202 us
    unnamed x12, waiting for transfers between devices  136 us
    all_gather x1, blocking collectives, gather_third(): return lax.all_gather(piece, ('rows', 'cols'), axis=0, tiled=True)  68.2 us
    all_gather x2, blocking collectives, per_device(): whole_a = lax.all_gather(shard_a, 'cols', axis=1, tiled=True)  61.9 us
    all_gather x2, blocking collectives, per_device(): whole_b = lax.all_gather(shard_b, 'rows', axis=1, tiled=True)  11.7 us
  transfers between devices with their start and end apart: 8, of which 7 were waited for; matrix products, arithmetic and copies ran while one was open for 2% of the time, Pallas kernels for 0%

profile of v1, /device:TPU:0, one launch (start us, length us, event | category | flops | bytes accessed | tf_op | source)
XLA Modules:
  0.0 514.7 jit_solution(14569483850213852325)
XLA Ops:
  7.2 6.5 %all-gather.1 = f32[4,64,32]{1,2,0:T(8,128)S(1)} all-gather(f32[1,64,32]{1,2,0:T(8,128)} %bitcast.87), channel_id=1, replica_groups=mesh['rows'=4,'cols'=8] {'rows'}, dimensions={0}, use_global_device_ids=true | all-gather | bytes 40960 | tf_op jit(solution)/shard_map/all_gather | solution.py:26
  14.4 31.3 %all-gather = f32[8,32,12]{1,2,0:T(8,128)S(1)} all-gather(f32[1,32,12]{1,2,0:T(8,128)S(1)} %bitcast.90), channel_id=1, replica_groups=mesh['rows'=4,'cols'=8] {'cols'}, dimensions={0}, use_global_device_ids=true | all-gather | bytes 13824 | tf_op jit(solution)/shard_map/all_gather | solution.py:25
  46.5 68.2 %all_gather.17 = f32[512,256]{1,0:T(8,128)S(1)} all-gather(f32[16,256]{1,0:T(8,128)S(1)} %copy-done.2), channel_id=1, replica_groups=mesh['rows'=4,'cols'=8] {'rows','cols'}, dimensions={0}, use_global_device_ids=true | all-gather | bytes 540672 | tf_op jit(solution)/shard_map/all_gather | solution.py:10
  114.7 0.9 fusion.7
  115.7 0.8 fusion.10
  118.2 2.2 fusion.11
  120.5 55.8 %reduce-scatter.13.cloned.1.call-done = f32[32,12]{1,0:T(8,128)} async-done(((f32[256,12]{1,0:T(8,128)}), f32[32,12]{1,0:T(8,128)}) %reduce-scatter.13.cloned.1.call-update) | async-done | bytes 1552
  176.4 0.8 copy.43
  177.2 30.5 %all-gather.3 = f32[8,32,12]{1,2,0:T(8,128)S(1)} all-gather(f32[1,32,12]{1,2,0:T(8,128)S(1)} %fusion.9), channel_id=1, replica_groups=mesh['rows'=4,'cols'=8] {'cols'}, dimensions={0}, use_global_device_ids=true | all-gather | bytes 13824 | tf_op jit(solution)/shard_map/all_gather | solution.py:25
  207.8 0.8 copy.45
  208.7 65.0 %all-reduce.5.cloned.1.call-done = f32[512,256]{1,0:T(8,128)} async-done(((f32[512,256]{1,0:T(8,128)}), f32[512,256]{1,0:T(8,128)}) %all-reduce.5.cloned.1.call-update) | async-done | bytes 524304 | tf_op jit(solution)/shard_map/psum | solution.py:48
  274.4 5.2 %all-gather.2 = f32[4,64,32]{1,2,0:T(8,128)S(1)} all-gather(f32[1,64,32]{1,2,0:T(8,128)S(1)} %fusion.8), channel_id=1, replica_groups=mesh['rows'=4,'cols'=8] {'rows'}, dimensions={0}, use_global_device_ids=true | all-gather | bytes 40960 | tf_op jit(solution)/shard_map/all_gather | solution.py:26
  279.8 28.7 %all-reduce.7.cloned.1.call-done = f32[512,256]{1,0:T(8,128)} async-done(((f32[512,256]{1,0:T(8,128)}), f32[512,256]{1,0:T(8,128)}) %all-reduce.7.cloned.1.call-update) | async-done | bytes 524304 | tf_op jit(solution)/shard_map/psum | solution.py:48
  308.5 1.1 multiply_subtract_fusion
  309.6 0.9 fusion.6
  310.5 0.8 fusion.12
  312.2 2.2 fusion.13
  315.4 58.9 %reduce-scatter.17.cloned.1.call-done = f32[32,12]{1,0:T(8,128)} async-done(((f32[256,12]{1,0:T(8,128)}), f32[32,12]{1,0:T(8,128)}) %reduce-scatter.17.cloned.1.call-update) | async-done | bytes 1552
  374.4 0.8 copy.47
  375.2 74.2 %all-reduce.9.cloned.1.call-done = f32[512,256]{1,0:T(8,128)} async-done(((f32[512,256]{1,0:T(8,128)}), f32[512,256]{1,0:T(8,128)}) %all-reduce.9.cloned.1.call-update) | async-done | bytes 524304 | tf_op jit(solution)/shard_map/psum | solution.py:48
  450.0 20.7 %reduce-scatter.19.cloned.1.call-done = f32[64,32]{1,0:T(8,128)} async-done(((f32[256,32]{1,0:T(8,128)}), f32[64,32]{1,0:T(8,128)}) %reduce-scatter.19.cloned.1.call-update) | async-done | bytes 8208
  470.7 0.8 copy.49
  472.1 34.4 %all-reduce.11.cloned.1.call-done = f32[512,256]{1,0:T(8,128)} async-done(((f32[512,256]{1,0:T(8,128)}), f32[512,256]{1,0:T(8,128)}) %all-reduce.11.cloned.1.call-update) | async-done | bytes 524304 | tf_op jit(solution)/shard_map/psum | solution.py:48
  506.5 1.3 dynamic-slice_subtract_fusion
  (47 shorter events, 7.3 us)
Async XLA Ops:
  7.2 169.2 %reduce-scatter.13.cloned.1.call-start = ((), (), s32[]{:S(2)}) async-start(), calls=%async_computation.8 | async-start | bytes 147456
  13.7 0.7 copy-start.1
  45.8 0.7 copy-start.2
  45.8 68.9 %copy-start.3 = (f32[12,32,512]{2,1,0:T(8,128)S(1)}, f32[12,32,512]{2,1,0:T(8,128)}, u32[]{:S(2)}) copy-start(f32[12,32,512]{2,1,0:T(8,128)} %param.4) | copy-start | bytes 2359300
  117.3 90.5 %reduce-scatter.15.cloned.1.call-start = ((), (), s32[]{:S(2)}) async-start(), calls=%async_computation.9 | async-start | bytes 163840
  118.2 155.5 %all-reduce.5.cloned.1.call-start = ((), (), s32[]{:S(2)}) async-start(), calls=%async_computation.4 | async-start | bytes 1048576 | tf_op jit(solution)/shard_map/psum | solution.py:48
  120.5 188.0 %all-reduce.7.cloned.1.call-start = ((), (), s32[]{:S(2)}) async-start(), calls=%async_computation.5 | async-start | bytes 1048576 | tf_op jit(solution)/shard_map/psum | solution.py:48
  273.7 0.7 copy-start
  273.7 100.7 %reduce-scatter.17.cloned.1.call-start = ((), (), s32[]{:S(2)}) async-start(), calls=%async_computation.10 | async-start | bytes 147456
  312.2 137.2 %all-reduce.9.cloned.1.call-start = ((), (), s32[]{:S(2)}) async-start(), calls=%async_computation.6 | async-start | bytes 1048576 | tf_op jit(solution)/shard_map/psum | solution.py:48
  314.5 156.2 %reduce-scatter.19.cloned.1.call-start = ((), (), s32[]{:S(2)}) async-start(), calls=%async_computation.11 | async-start | bytes 163840
  315.4 191.1 %all-reduce.11.cloned.1.call-start = ((), (), s32[]{:S(2)}) async-start(), calls=%async_computation.7 | async-start | bytes 1048576 | tf_op jit(solution)/shard_map/psum | solution.py:48
Sparse Core Ops, SparseCore 0:
  117.4 58.9 reduce-scatter.12
  178.8 18.6 reduce-scatter.14
  200.9 72.6 all-reduce.4
  275.9 32.5 all-reduce.6
  312.3 62.0 reduce-scatter.16
  377.7 71.6 all-reduce.8
  451.8 18.8 reduce-scatter.18
  473.0 33.4 all-reduce.10

commit v2 on v0

--- a/solution.py
+++ b/solution.py
@@ -6,8 +6,20 @@
 STEPS = 2
 
 
+def doubled_up(x, axis, dim):
+    ways, here = (lax.axis_size(axis), lax.axis_index(axis))
+    grown, reach = (x, 1)
+    while reach < ways:
+        theirs = lax.ppermute(grown, axis, [(d, d ^ reach) for d in range(ways)])
+        mine_first = jnp.concatenate([grown, theirs], axis=dim)
+        theirs_first = jnp.concatenate([theirs, grown], axis=dim)
+        grown = jnp.where(here & reach == 0, mine_first, theirs_first)
+        reach = 2 * reach
+    return grown
+
+
 def gather_third(piece):
-    return lax.all_gather(piece, ("rows", "cols"), axis=0, tiled=True)
+    return doubled_up(piece, ("rows", "cols"), 0)
 
 
 def per_device(tensor, first_factor, second_factor, third_factor):

time: 397 us -> 352 us (0.89)
  blocking collectives: 142 us -> 75.3 us
  waiting for transfers between devices: 219 us -> 231 us
  starting transfers between devices: 0.25 us -> 10.5 us
    all_gather x1 -> x0, blocking collectives: 68.2 us -> none  [gather_third(): return lax.all_gather(piece, ('rows', 'cols'), axis=0, tiled=True)]
    ppermute x0 -> x5, starting transfers between devices: none -> 10.3 us  [doubled_up(): theirs = lax.ppermute(grown, axis, [(d, d ^ reach) for d in range(ways)])]
    ppermute x0 -> x5, waiting for transfers between devices: none -> 7.4 us  [doubled_up(): theirs = lax.ppermute(grown, axis, [(d, d ^ reach) for d in range(ways)])]
  transfers between devices with their start and end apart: 6 -> 11, of which waited for: 5 -> 9; matrix products, arithmetic and copies ran while one was open for 3% -> 3% of each run, Pallas kernels for 0% -> 0%
where the time goes in v2:
time: 352 us; the launch traced here: 351 us
  waiting for transfers between devices  231 us (66%)
  blocking collectives  75.3 us (21%)
  between operations  15.4 us (4%)
  starting transfers between devices  10.5 us (3%)
  matrix products  7.99 us (2%)
  local copies, waits for them, and re-layouts  7.35 us (2%)
  other arithmetic  4.02 us (1%)
    unnamed x10, waiting for transfers between devices  137 us
    psum x2, waiting for transfers between devices, per_device(): whole_c = whole_c - rate_c * lax.psum(term_c, ('rows', 'cols'))  85.9 us
    all_gather x2, blocking collectives, per_device(): whole_a = lax.all_gather(shard_a, 'cols', axis=1, tiled=True)  62.3 us
    all_gather x2, blocking collectives, per_device(): whole_b = lax.all_gather(shard_b, 'rows', axis=1, tiled=True)  13 us
    ppermute x5, starting transfers between devices, doubled_up(): theirs = lax.ppermute(grown, axis, [(d, d ^ reach) for d in range(ways)])  10.3 us
    ppermute x5, waiting for transfers between devices, doubled_up(): theirs = lax.ppermute(grown, axis, [(d, d ^ reach) for d in range(ways)])  7.4 us
    unnamed x20, local copies, waits for them, and re-layouts  7.23 us
  transfers between devices with their start and end apart: 11, of which 9 were waited for; matrix products, arithmetic and copies ran while one was open for 3% of the time, Pallas kernels for 0%

profile of v2, /device:TPU:0, one launch (start us, length us, event | category | flops | bytes accessed | tf_op | source)
XLA Modules:
  0.0 351.2 jit_solution(11944969352527034032)
XLA Ops:
  8.1 3.1 collective-permute-start
  11.1 1.9 collective-permute-done
  13.1 2.1 collective-permute-start.1
  15.2 1.9 collective-permute-done.1
  17.1 3.1 collective-permute-start.2
  20.2 2.2 collective-permute-done.2
  22.5 1.3 collective-permute-done.3
  23.9 1.9 collective-permute-start.4
  25.8 7.8 %all-gather.1 = f32[4,64,32]{1,2,0:T(8,128)S(1)} all-gather(f32[1,64,32]{1,2,0:T(8,128)S(1)} %bitcast.85), channel_id=1, replica_groups=mesh['rows'=4,'cols'=8] {'rows'}, dimensions={0}, use_global_device_ids=true | all-gather | bytes 40960 | tf_op jit(solution)/shard_map/all_gather | solution.py:38
  34.3 31.7 %all-gather = f32[8,32,12]{1,2,0:T(8,128)S(1)} all-gather(f32[1,32,12]{1,2,0:T(8,128)S(1)} %bitcast.88), channel_id=1, replica_groups=mesh['rows'=4,'cols'=8] {'cols'}, dimensions={0}, use_global_device_ids=true | all-gather | bytes 13824 | tf_op jit(solution)/shard_map/all_gather | solution.py:37
  66.2 1.0 fusion.7
  69.7 2.3 fusion.13
  72.1 59.8 %reduce-scatter.13.cloned.1.call-done = f32[32,12]{1,0:T(8,128)} async-done(((f32[256,12]{1,0:T(8,128)}), f32[32,12]{1,0:T(8,128)}) %reduce-scatter.13.cloned.1.call-update) | async-done | bytes 1552
  132.7 30.6 %all-gather.3 = f32[8,32,12]{1,2,0:T(8,128)S(1)} all-gather(f32[1,32,12]{1,2,0:T(8,128)S(1)} %fusion.10), channel_id=1, replica_groups=mesh['rows'=4,'cols'=8] {'cols'}, dimensions={0}, use_global_device_ids=true | all-gather | bytes 13824 | tf_op jit(solution)/shard_map/all_gather | solution.py:37
  163.3 0.8 copy.45
  164.2 5.2 %all-gather.2 = f32[4,64,32]{1,2,0:T(8,128)S(1)} all-gather(f32[1,64,32]{1,2,0:T(8,128)S(1)} %fusion.9), channel_id=1, replica_groups=mesh['rows'=4,'cols'=8] {'rows'}, dimensions={0}, use_global_device_ids=true | all-gather | bytes 40960 | tf_op jit(solution)/shard_map/all_gather | solution.py:38
  169.6 35.2 %all-reduce.3.cloned.1.call-done = f32[512,256]{1,0:T(8,128)} async-done(((f32[512,256]{1,0:T(8,128)}), f32[512,256]{1,0:T(8,128)}) %all-reduce.3.cloned.1.call-update) | async-done | bytes 524304 | tf_op jit(solution)/shard_map/psum | solution.py:60
  204.8 1.2 multiply_subtract_fusion
  206.0 0.9 fusion.6
  209.5 2.2 fusion.15
  211.7 58.0 %reduce-scatter.17.cloned.1.call-done = f32[32,12]{1,0:T(8,128)} async-done(((f32[256,12]{1,0:T(8,128)}), f32[32,12]{1,0:T(8,128)}) %reduce-scatter.17.cloned.1.call-update) | async-done | bytes 1552
  271.1 19.5 %reduce-scatter.19.cloned.1.call-done = f32[64,32]{1,0:T(8,128)} async-done(((f32[256,32]{1,0:T(8,128)}), f32[64,32]{1,0:T(8,128)}) %reduce-scatter.19.cloned.1.call-update) | async-done | bytes 8208
  292.1 50.7 %all-reduce.5.cloned.1.call-done = f32[512,256]{1,0:T(8,128)} async-done(((f32[512,256]{1,0:T(8,128)}), f32[512,256]{1,0:T(8,128)}) %all-reduce.5.cloned.1.call-update) | async-done | bytes 524304 | tf_op jit(solution)/shard_map/psum | solution.py:60
  342.8 1.3 dynamic-slice_subtract_fusion
  (54 shorter events, 10.1 us)
Async XLA Ops:
  8.0 5.0 %copy-start.2 = (f32[16,256]{1,0:T(8,128)S(1)}, f32[16,256]{1,0:T(8,128)}, u32[]{:S(2)}) copy-start(f32[16,256]{1,0:T(8,128)} %param.7) | copy-start | bytes 49156
  8.0 123.8 %reduce-scatter.13.cloned.1.call-start = ((), (), s32[]{:S(2)}) async-start(), calls=%async_computation.6 | async-start | bytes 147456
  8.1 5.0 %collective-permute-start = (f32[16,256]{1,0:T(8,128)}, f32[16,256]{1,0:T(8,128)S(1)}, u32[]{:S(2)}, u32[]{:S(2)}) collective-permute-start(f32[16,256]{1,0:T(8,128)} %param.7), channel_id=1, source_target_pairs={{0,1},{1,0},{2,3},{3,2},{4,5},{5,4},{6,7},{7,6},{8,9},{9,8},{10,11... | collective-permute-start | bytes 49160 | tf_op jit(solution)/shard_map/ppermute | solution.py:13
  13.1 4.0 %collective-permute-start.1 = (f32[32,256]{1,0:T(8,128)S(1)}, f32[32,256]{1,0:T(8,128)S(1)}, u32[]{:S(2)}, u32[]{:S(2)}) collective-permute-start(f32[32,256]{1,0:T(8,128)S(1)} %maximum_select_fusion.6), channel_id=1, source_target_pairs={{0,2},{1,3},{2,0},{3,1},{4,6},{5,7},{6,4},{7,5},{8,10},{9,11},{10,... | collective-permute-start | bytes 98312 | tf_op jit(solution)/shard_map/ppermute | solution.py:13
  17.1 5.3 %collective-permute-start.2 = (f32[64,256]{1,0:T(8,128)S(1)}, f32[64,256]{1,0:T(8,128)S(1)}, u32[]{:S(2)}, u32[]{:S(2)}) collective-permute-start(f32[64,256]{1,0:T(8,128)S(1)} %maximum_select_fusion.5), channel_id=1, source_target_pairs={{0,4},{1,5},{2,6},{3,7},{4,0},{5,1},{6,2},{7,3},{8,12},{9,13},{10,... | collective-permute-start | bytes 196616 | tf_op jit(solution)/shard_map/ppermute | solution.py:13
  22.4 43.7 %copy-start.3 = (f32[12,32,512]{2,1,0:T(8,128)S(1)}, f32[12,32,512]{2,1,0:T(8,128)}, u32[]{:S(2)}) copy-start(f32[12,32,512]{2,1,0:T(8,128)} %param.4) | copy-start | bytes 2359300
  22.5 1.4 collective-permute-start.3
  23.9 1.9 copy-start
  23.9 42.3 %collective-permute-start.4 = (f32[256,256]{1,0:T(8,128)S(1)}, f32[256,256]{1,0:T(8,128)S(1)}, u32[]{:S(2)}, u32[]{:S(2)}) collective-permute-start(f32[256,256]{1,0:T(8,128)S(1)} %maximum_select_fusion.1), channel_id=1, source_target_pairs={{0,16},{1,17},{2,18},{3,19},{4,20},{5,21},{6,22},{7,23},{8,24},{9,... | collective-permute-start | bytes 786440 | tf_op jit(solution)/shard_map/ppermute | solution.py:13
  33.6 0.7 copy-start.1
  68.8 94.5 %reduce-scatter.15.cloned.1.call-start = ((), (), s32[]{:S(2)}) async-start(), calls=%async_computation.7 | async-start | bytes 163840
  69.7 135.1 %all-reduce.3.cloned.1.call-start = ((), (), s32[]{:S(2)}) async-start(), calls=%async_computation.4 | async-start | bytes 1048576 | tf_op jit(solution)/shard_map/psum | solution.py:60
  72.0 197.7 %reduce-scatter.17.cloned.1.call-start = ((), (), s32[]{:S(2)}) async-start(), calls=%async_computation.8 | async-start | bytes 147456
  208.6 82.1 %reduce-scatter.19.cloned.1.call-start = ((), (), s32[]{:S(2)}) async-start(), calls=%async_computation.9 | async-start | bytes 163840
  209.4 133.4 %all-reduce.5.cloned.1.call-start = ((), (), s32[]{:S(2)}) async-start(), calls=%async_computation.5 | async-start | bytes 1048576 | tf_op jit(solution)/shard_map/psum | solution.py:60
Sparse Core Ops, SparseCore 0:
  68.9 62.8 reduce-scatter.12
  134.3 18.6 reduce-scatter.14
  208.7 61.0 reduce-scatter.16
  272.0 18.6 reduce-scatter.18
Sparse Core Ops, SparseCore 1:
  75.4 129.3 all-reduce.2
  215.2 127.5 all-reduce.4
